TPU v7x, 32 devices: a whole 2x2x4 slice. The times are simulated.
32 devices in a mesh: slab: 2 (over y), gy: 4 (over z), gx: 4 (over x, core).
Axes of the slice: x: 2, y: 2, z: 4, core: 2. Of those that a mesh axis runs over, the one named last changes fastest.
Arguments:
- volume: float32 [8, 256, 1024], P(None, ('slab', 'gy'), 'gx'), parts along dimension 1, may hold values from -8 to 8
- tissue_mask: int32 [2, 32, 128], P(None, ('slab', 'gy'), 'gx'), parts along dimension 1, may hold values from 0 to 1
- smoothing: float32 [1], replicated, may hold values from 0.7 to 1.4
Outputs:
- filtered: float32 [8, 256, 1024], P(None, ('slab', 'gy'), 'gx'), parts along dimension 1
There are 2 independent parts, one for each index of `slab`. A program takes and returns all parts, laid end to end along the dimension named above; an argument that names none is the same for every part. Nothing has to cross between parts.
All inputs are finite; a program needn't handle non-finite values.
Results may differ from a plain program's by a relative error of at most 0.00002.
Values sent between devices are 32-bit elements; how exact they have to be, the bound alone decides.
A program may use at most 64 MiB of HBM per device.

v0:
```python
import jax
import jax.numpy as jnp
from jax import lax
from jax.sharding import PartitionSpec as P

OFFSETS = [(a, b, c) for a in (-4, 0, 4) for b in (-8, 0, 8) for c in (-8, 0, 8)]


def extended(block, sides, width):
    for axis, dim in sides:
        count = lax.axis_size(axis)
        forward = [(i, i + 1) for i in range(count - 1)]
        backward = [(target, source) for source, target in forward]
        low = lax.ppermute(
            lax.slice_in_dim(block, block.shape[dim] - width, None, axis=dim), axis, forward
        )
        high = lax.ppermute(lax.slice_in_dim(block, 0, width, axis=dim), axis, backward)
        block = jnp.concatenate([low, block, high], axis=dim)
    return block


def expand_mask(tissue_mask):
    blocks_z, blocks_y, blocks_x = tissue_mask.shape
    spread = jnp.broadcast_to(
        tissue_mask[:, None, :, None, :, None], (blocks_z, 4, blocks_y, 8, blocks_x, 8)
    )
    return spread.reshape(blocks_z * 4, blocks_y * 8, blocks_x * 8).astype(jnp.float32)


def noise_terms(values, tissue):
    residual = values[1:-1] - 0.5 * (values[:-2] + values[2:])
    inner = tissue[1:-1]
    summed = jnp.sum(inner * residual * residual) * (2.0 / 3.0)
    return (summed, jnp.sum(inner))


def box_sum(squared, depth, rows, cols):
    first = squared[0:depth] + squared[1 : depth + 1] + squared[2 : depth + 2]
    second = first[:, 0:rows] + first[:, 1 : rows + 1] + first[:, 2 : rows + 2]
    return second[:, :, 0:cols] + second[:, :, 1 : cols + 1] + second[:, :, 2 : cols + 2]


def smooth_once(padded_vals, padded_tiss, values, tissue, inverse_width):
    depth, rows, cols = values.shape
    centre = padded_vals[4 : depth + 6, 8 : rows + 10, 8 : cols + 10]
    numerator = jnp.zeros(values.shape, jnp.float32)
    denominator = jnp.zeros(values.shape, jnp.float32)
    for offset in OFFSETS:
        shift_z, shift_y, shift_x = offset
        moved = padded_vals[
            4 + shift_z : depth + 6 + shift_z,
            8 + shift_y : rows + 10 + shift_y,
            8 + shift_x : cols + 10 + shift_x,
        ]
        differ = centre - moved
        distance = box_sum(differ * differ, depth, rows, cols)
        other_tiss = padded_tiss[
            5 + shift_z : 5 + shift_z + depth,
            9 + shift_y : 9 + shift_y + rows,
            9 + shift_x : 9 + shift_x + cols,
        ]
        other_vals = padded_vals[
            5 + shift_z : 5 + shift_z + depth,
            9 + shift_y : 9 + shift_y + rows,
            9 + shift_x : 9 + shift_x + cols,
        ]
        weight_field = jnp.exp(-distance * inverse_width) * other_tiss
        numerator = numerator + weight_field * other_vals
        denominator = denominator + weight_field
    return tissue * numerator / (denominator + 1.0 - tissue) + (1.0 - tissue) * values


def widen_values(values):
    widened = extended(values, (("gy", 1), ("gx", 2)), 9)
    return jnp.pad(widened, ((5, 5), (0, 0), (0, 0)))


def on_device(volume, tissue_mask, smoothing):
    tissue = expand_mask(tissue_mask)
    local_sum, local_count = noise_terms(volume, tissue)
    summed, tissue_count = lax.psum((local_sum, local_count), ("gy", "gx"))
    variance = summed / jnp.maximum(tissue_count, 1.0) + 1e-05
    inverse_width = 1.0 / (54.0 * smoothing[0] * smoothing[0] * variance)
    stacked = jnp.stack([volume, tissue])
    widened = extended(stacked, (("gy", 2), ("gx", 3)), 9)
    widened = jnp.pad(widened, ((0, 0), (5, 5), (0, 0), (0, 0)))
    padded_tiss = widened[1]
    values = smooth_once(widened[0], padded_tiss, volume, tissue, inverse_width)
    padded_vals = widen_values(values)
    values = smooth_once(padded_vals, padded_tiss, values, tissue, inverse_width)
    return values


def solution(mesh):
    placed = (P(None, ("slab", "gy"), "gx"), P(None, ("slab", "gy"), "gx"), P())
    return jax.shard_map(
        on_device,
        mesh=mesh,
        in_specs=placed,
        out_specs=P(None, ("slab", "gy"), "gx"),
        check_vma=False,
    )
```

profile of v0, /device:TPU:0, one launch (start us, length us, event | category | flops | bytes accessed | tf_op | source)
XLA Modules:
  0.0 173.6 jit_solution(4089723964887068323)
XLA Ops:
  0.7 2.6 %broadcast_in_dim.2 = f32[2,4,4,8,32,8]{5,4,3,2,1,0:T(8,128)} broadcast(f32[2,4,32]{2,1,0:T(4,128)S(1)} %convert_element_type.22), dimensions={0,2,4} | broadcast | bytes 263168 | tf_op jit(solution)/shard_map/broadcast_in_dim | solution.py:24
  3.2 4.1 %convert_element_type.24 = f32[1,8,32,256]{3,2,1,0:T(8,128)S(1)} reshape(f32[2,4,4,8,32,8]{5,4,3,2,1,0:T(8,128)} %broadcast_in_dim.2) | data formatting | bytes 524288 | tf_op jit(solution)/shard_map/convert_element_type | solution.py:27
  7.4 5.0 %collective-permute-start = (f32[2,8,9,256]{3,2,1,0:T(8,128)S(1)}, f32[2,8,9,256]{3,2,1,0:T(8,128)S(1)}, u32[]{:S(2)}, u32[]{:S(2)}) collective-permute-start(f32[2,8,9,256]{3,2,1,0:T(8,128)S(1)} %get-tuple-element.69), channel_id=1, source_target_pairs={{0,4},{4,8},{8,12},{1,5},{5,9},{9,13},{2,6},{6,10},{10,14},{3,7},{... | collective-permute-start | bytes 442376 | tf_op jit(solution)/shard_map/ppermute | solution.py:14
  12.4 1.3 collective-permute-start.1
  13.7 4.0 %convert_element_type.23 = f32[8,32,256]{2,1,0:T(8,128)S(1)} reshape(f32[2,4,4,8,32,8]{5,4,3,2,1,0:T(8,128)} %broadcast_in_dim.2) | data formatting | bytes 524288 | tf_op jit(solution)/shard_map/convert_element_type | solution.py:27
  17.9 4.1 %collective-permute-done.1 = f32[2,8,9,256]{3,2,1,0:T(8,128)S(1)} collective-permute-done((f32[2,8,9,256]{3,2,1,0:T(8,128)S(1)}, f32[2,8,9,256]{3,2,1,0:T(8,128)S(1)}, u32[]{:S(2)}, u32[]{:S(2)}) %collective-permute-start.1) | collective-permute-done | bytes 147488 | tf_op jit(solution)/shard_map/ppermute | solution.py:17
  22.3 1.3 collective-permute-start.2
  23.7 1.3 collective-permute-start.3
  26.3 34.1 %all-reduce.2 = (f32[]{:T(128)}, f32[]{:T(128)}) all-reduce(f32[]{:T(128)S(6)} %mul.743, f32[]{:T(128)} %get-tuple-element.5), channel_id=1, replica_groups=mesh['slab'=2,'gy'=4,'gx'=4] {'gy','gx'}, use_global_device_ids=true, to_apply=%region_1.0 | all-reduce | flops 2 | bytes 16 | tf_op jit(solution)/shard_map/psum | solution.py:81
  62.4 1.4 select_maximum_fusion
  64.1 1.0 fusion.51
  65.1 1.2 fusion.53
  66.3 1.2 fusion.52
  68.4 0.8 slice_add_fusion.210
  69.3 0.8 slice_add_fusion.182
  70.2 0.9 slice_add_fusion.184
  72.0 0.9 slice_add_fusion.206
  72.9 0.8 slice_add_fusion.162
  74.6 0.8 slice_add_fusion.214
  75.6 0.8 slice_add_fusion.178
  78.2 0.8 slice_add_fusion.200
  79.1 0.8 slice_add_fusion.164
  79.9 0.9 slice_add_fusion.170
  80.9 0.9 slice_add_fusion.202
  81.8 0.9 slice_add_fusion.204
  82.7 0.8 slice_add_fusion.196
  83.6 0.9 slice_add_fusion.212
  84.5 0.8 slice_add_fusion.166
  85.3 0.8 slice_add_fusion.168
  86.3 0.9 slice_add_fusion.174
  88.0 0.8 slice_add_fusion.188
  90.6 0.8 slice_add_fusion.194
  91.5 18.5 %fusion.197 = f32[8,32,256]{2,1,0:T(8,128)} fusion(f32[8,32,256]{2,1,0:T(8,128)} %copy-done.2, f32[18,50,274]{2,1,0:T(8,128)S(1)} %get-tuple-element.10, f32[8,32,256]{2,1,0:T(8,128)S(1)} %copy-done, f32[8,32,258]{2,1,0:T(8,128)} %slice_add_fusion.162, f32[8,32,258]{2,1,0:T(8,128)} %slice_add_fusion.164, f32[8,32,258]{2,1,0:T(8,128)} %slice_add_fusion.166, ...), kind=kLoop, calls=%fused_computation.570 | loop fusion | flops 14483456 | bytes 36175876 | tf_op jit(solution)/shard_map/add | solution.py:70
  110.0 1.0 fusion.334
  111.0 1.3 collective-permute-start.4
  112.3 1.3 collective-permute-start.5
  113.6 1.2 collective-permute-done.4
  114.8 4.4 %collective-permute-done.5 = f32[8,9,256]{2,1,0:T(8,128)S(1)} collective-permute-done((f32[8,9,256]{2,1,0:T(8,128)S(1)}, f32[8,9,256]{2,1,0:T(8,128)S(1)}, u32[]{:S(2)}, u32[]{:S(2)}) %collective-permute-start.5) | collective-permute-done | bytes 73760 | tf_op jit(solution)/shard_map/ppermute | solution.py:17
  119.2 1.0 pad_maximum_fusion.2
  120.3 1.3 collective-permute-start.6
  121.7 1.6 collective-permute-start.7
  123.2 1.8 %collective-permute-done.7 = f32[8,50,9]{2,1,0:T(8,128)S(1)} collective-permute-done((f32[8,50,9]{2,1,0:T(8,128)S(1)}, f32[8,50,9]{2,1,0:T(8,128)S(1)}, u32[]{:S(2)}, u32[]{:S(2)}) %collective-permute-start.7) | collective-permute-done | bytes 14432 | tf_op jit(solution)/shard_map/ppermute | solution.py:17
  125.4 1.0 fusion.27
  126.4 1.2 fusion.26
  127.6 1.2 subtract_multiply_fusion
  130.6 0.8 slice_add_fusion.114
  131.5 0.9 slice_add_fusion.154
  132.4 0.8 slice_add_fusion.122
  133.3 0.8 slice_add_fusion.156
  134.1 0.8 slice_add_fusion.108
  135.0 0.8 slice_add_fusion.124
  136.8 0.9 slice_add_fusion.144
  138.6 0.9 slice_add_fusion.146
  140.3 0.8 slice_add_fusion.148
  142.1 0.8 slice_add_fusion.150
  144.7 0.9 slice_add_fusion.126
  145.6 0.8 slice_add_fusion.128
  146.5 0.8 slice_add_fusion.130
  147.4 0.8 slice_add_fusion.132
  148.3 0.8 slice_add_fusion.136
  150.9 0.9 slice_add_fusion.142
  151.9 0.9 slice_add_fusion.116
  152.7 1.4 maximum_maximum_fusion
  154.1 19.3 %fusion.58 = f32[8,32,256]{2,1,0:T(8,128)} fusion(f32[8,32,256]{2,1,0:T(8,128)} %copy-done.2, f32[18,50,274]{2,1,0:T(8,128)S(1)} %select_maximum_fusion.5, f32[8,50,265]{2,1,0:T(8,128)} %get-tuple-element.68, f32[8,9,256]{2,1,0:T(8,128)} %copy-done.3, f32[8,32,256]{2,1,0:T(8,128)S(1)} %copy-done.1, f32[8,50,265]{2,1,0:T(8,128)} %get-tuple-element.67, ...), kind=kLoop, calls=%fused_computation.351 | loop fusion | flops 14614528 | bytes 35536900 | tf_op jit(solution)/shard_map/add | solution.py:70
  (79 shorter events, 19.9 us)
Async XLA Ops:
  3.2 4.1 %copy-start = (f32[8,32,256]{2,1,0:T(8,128)S(1)}, f32[8,32,256]{2,1,0:T(8,128)}, u32[]{:S(2)}) copy-start(f32[8,32,256]{2,1,0:T(8,128)} %param.3) | copy-start | bytes 786436
  7.4 10.5 %collective-permute-start = (f32[2,8,9,256]{3,2,1,0:T(8,128)S(1)}, f32[2,8,9,256]{3,2,1,0:T(8,128)S(1)}, u32[]{:S(2)}, u32[]{:S(2)}) collective-permute-start(f32[2,8,9,256]{3,2,1,0:T(8,128)S(1)} %get-tuple-element.69), channel_id=1, source_target_pairs={{0,4},{4,8},{8,12},{1,5},{5,9},{9,13},{2,6},{6,10},{10,14},{3,7},{... | collective-permute-start | bytes 442376 | tf_op jit(solution)/shard_map/ppermute | solution.py:14
  12.4 9.7 %collective-permute-start.1 = (f32[2,8,9,256]{3,2,1,0:T(8,128)S(1)}, f32[2,8,9,256]{3,2,1,0:T(8,128)S(1)}, u32[]{:S(2)}, u32[]{:S(2)}) collective-permute-start(f32[2,8,9,256]{3,2,1,0:T(8,128)S(1)} %get-tuple-element.70), channel_id=1, source_target_pairs={{4,0},{8,4},{12,8},{5,1},{9,5},{13,9},{6,2},{10,6},{14,10},{7,3},{... | collective-permute-start | bytes 442376 | tf_op jit(solution)/shard_map/ppermute | solution.py:17
  17.7 7.3 %copy-start.2 = (f32[8,32,256]{2,1,0:T(8,128)}, f32[8,32,256]{2,1,0:T(8,128)S(1)}, u32[]{:S(2)}) copy-start(f32[8,32,256]{2,1,0:T(8,128)S(1)} %convert_element_type.23) | copy-start | bytes 786436
  22.3 40.1 %collective-permute-start.2 = (f32[2,8,50,9]{3,2,1,0:T(8,128)S(1)}, f32[2,8,50,9]{3,2,1,0:T(8,128)S(1)}, u32[]{:S(2)}, u32[]{:S(2)}) collective-permute-start(f32[2,8,50,9]{3,2,1,0:T(8,128)S(1)} %get-tuple-element.65), channel_id=1, source_target_pairs={{0,1},{1,2},{2,3},{4,5},{5,6},{6,7},{8,9},{9,10},{10,11},{12,13},{... | collective-permute-start | bytes 86408 | tf_op jit(solution)/shard_map/ppermute | solution.py:14
  23.7 38.7 %collective-permute-start.3 = (f32[2,8,50,9]{3,2,1,0:T(8,128)S(1)}, f32[2,8,50,9]{3,2,1,0:T(8,128)S(1)}, u32[]{:S(2)}, u32[]{:S(2)}) collective-permute-start(f32[2,8,50,9]{3,2,1,0:T(8,128)S(1)} %get-tuple-element.66), channel_id=1, source_target_pairs={{1,0},{2,1},{3,2},{5,4},{6,5},{7,6},{9,8},{10,9},{11,10},{13,12},{... | collective-permute-start | bytes 86408 | tf_op jit(solution)/shard_map/ppermute | solution.py:17
  110.0 15.1 %copy-start.1 = (f32[8,32,256]{2,1,0:T(8,128)S(1)}, f32[8,32,256]{2,1,0:T(8,128)}, u32[]{:S(2)}) copy-start(f32[8,32,256]{2,1,0:T(8,128)} %fusion.197) | copy-start | bytes 786436
  111.0 3.8 %collective-permute-start.4 = (f32[8,9,256]{2,1,0:T(8,128)S(1)}, f32[8,9,256]{2,1,0:T(8,128)S(1)}, u32[]{:S(2)}, u32[]{:S(2)}) collective-permute-start(f32[8,9,256]{2,1,0:T(8,128)S(1)} %get-tuple-element.73), channel_id=1, source_target_pairs={{0,4},{4,8},{8,12},{1,5},{5,9},{9,13},{2,6},{6,10},{10,14},{3,7},{... | collective-permute-start | bytes 221192 | tf_op jit(solution)/shard_map/ppermute | solution.py:14
  112.3 6.9 %collective-permute-start.5 = (f32[8,9,256]{2,1,0:T(8,128)S(1)}, f32[8,9,256]{2,1,0:T(8,128)S(1)}, u32[]{:S(2)}, u32[]{:S(2)}) collective-permute-start(f32[8,9,256]{2,1,0:T(8,128)S(1)} %get-tuple-element.74), channel_id=1, source_target_pairs={{4,0},{8,4},{12,8},{5,1},{9,5},{13,9},{6,2},{10,6},{14,10},{7,3},{... | collective-permute-start | bytes 221192 | tf_op jit(solution)/shard_map/ppermute | solution.py:17
  119.2 33.5 %copy-start.3 = (f32[8,9,256]{2,1,0:T(8,128)}, f32[8,9,256]{2,1,0:T(8,128)S(1)}, u32[]{:S(2)}) copy-start(f32[8,9,256]{2,1,0:T(8,128)S(1)} %collective-permute-done.5) | copy-start | bytes 221188
  120.3 2.9 %collective-permute-start.6 = (f32[8,50,9]{2,1,0:T(8,128)S(1)}, f32[8,50,9]{2,1,0:T(8,128)S(1)}, u32[]{:S(2)}, u32[]{:S(2)}) collective-permute-start(f32[8,50,9]{2,1,0:T(8,128)S(1)} %get-tuple-element.71), channel_id=1, source_target_pairs={{0,1},{1,2},{2,3},{4,5},{5,6},{6,7},{8,9},{9,10},{10,11},{12,13},{... | collective-permute-start | bytes 43208 | tf_op jit(solution)/shard_map/ppermute | solution.py:14
  121.7 3.4 %collective-permute-start.7 = (f32[8,50,9]{2,1,0:T(8,128)S(1)}, f32[8,50,9]{2,1,0:T(8,128)S(1)}, u32[]{:S(2)}, u32[]{:S(2)}) collective-permute-start(f32[8,50,9]{2,1,0:T(8,128)S(1)} %get-tuple-element.72), channel_id=1, source_target_pairs={{1,0},{2,1},{3,2},{5,4},{6,5},{7,6},{9,8},{10,9},{11,10},{13,12},{... | collective-permute-start | bytes 43208 | tf_op jit(solution)/shard_map/ppermute | solution.py:17
where the time goes:
time: 175 us; the launch traced here: 174 us
  other arithmetic  98 us (56%)
  blocking collectives  34.1 us (19%)
  starting transfers between devices  14.3 us (8%)
  local copies, waits for them, and re-layouts  12.2 us (7%)
  waiting for transfers between devices  11.7 us (7%)
  between operations  3.22 us (2%)
    add x54, other arithmetic, box_sum(): second = first[:, 0:rows] + first[:, 1:rows + 1] + first[:, 2:rows + 2]  45.3 us
    add x2, other arithmetic, smooth_once(): tissue * numerator / (denominator + 1.0 - tissue) + (1.0 - tissue) * values  37.7 us
    psum x1, blocking collectives, on_device(): summed, tissue_count = lax.psum((local_sum, local_count), ('gy', 'gx'))  34.1 us
    ppermute x4, waiting for transfers between devices, extended(): lax.ppermute(lax.slice_in_dim(block, 0, width, axis=dim), axis, backward)  10.3 us
    ppermute x4, starting transfers between devices, extended(): lax.ppermute(lax.slice_in_dim(block, block.shape[dim] - width, None, axis...  8.89 us
    convert_element_type x2, local copies, waits for them, and re-layouts, expand_mask(): spread.reshape(blocks_z * 4, blocks_y * 8, blocks_x * 8).astype(jnp.float32)  8.09 us
    mul x6, other arithmetic, smooth_once(): distance = box_sum(differ * differ, depth, rows, cols)  6.78 us
    ppermute x4, starting transfers between devices, extended(): lax.ppermute(lax.slice_in_dim(block, 0, width, axis=dim), axis, backward)  5.43 us
  transfers between devices with their start and end apart: 8, of which 5 were waited for; matrix products, arithmetic and copies ran while one was open for 3% of the time, Pallas kernels for 0%

commit v1 on v0

v1 whole, which is shorter than its diff:
```python
import functools

import jax
import jax.numpy as jnp
from jax import lax
from jax.experimental import pallas as pl
from jax.experimental.pallas import tpu as pltpu
from jax.sharding import PartitionSpec as P

MESH = pl.DeviceIdType.MESH
ITERS = 2
SHIFTS = (-9, -8, -7, -1, 0, 1, 7, 8, 9)
DIRS = ((1, 0), (-1, 0), (0, 1), (0, -1), (1, 1), (1, -1), (-1, 1), (-1, -1))


def kernel(
    ny, nx, smooth_ref, vol_ref, mask_ref, out_ref,
    mid, base, shifted, tissue, tissvals, numer, denom, own_tiss, near_tiss, wide_tiss,
    rows_in, row_in, row_out, pack_out, pack_in, corner_in, edge, sums,
    sum_send, sum_recv, halo_send, halo_recv,
):
    depth, rows, cols = vol_ref.shape
    lanes = 128
    tiles = cols // lanes
    blocks_z, blocks_y, blocks_x = mask_ref.shape
    padded = shifted.shape[3]
    peers = ny * nx
    gy, gx = lax.axis_index("gy"), lax.axis_index("gx")
    me = gy * nx + gx

    barrier = pltpu.get_barrier_semaphore()
    for k in range(1, peers):
        flat = lax.rem(me + k, peers)
        pl.semaphore_signal(
            barrier, inc=1, device_id={"gy": flat // nx, "gx": lax.rem(flat, nx)}, device_id_type=MESH
        )

    def exists(dy, dx):
        found = None
        for step, pos, count in ((dy, gy, ny), (dx, gx, nx)):
            if step == 0:
                continue
            here = pos < count - 1 if step > 0 else pos > 0
            found = here if found is None else jnp.logical_and(found, here)
        return found

    def lane_group(shape):
        return lax.broadcasted_iota(jnp.int32, shape, 1) // 16

    def make_packs(src, it):
        group = lane_group((rows, lanes))
        right = jnp.zeros((rows, lanes), jnp.float32)
        left = right
        for z in range(depth):
            high = pltpu.roll(src[z, :, cols - lanes : cols], (16 * z + 16) % lanes, 1)
            right = jnp.where(group == z, high, right)
            low = src[z, :, 0:lanes]
            if z:
                low = pltpu.roll(low, 16 * z, 1)
            left = jnp.where(group == z, low, left)
            row_out[it, 0, z : z + 1] = src[z, rows - 9 : rows - 8, :]
            row_out[it, 1, z : z + 1] = src[z, 8:9, :]
        pack_out[it, 0] = right
        pack_out[it, 1] = left

    def copies(src, it, d):
        dy, dx = DIRS[d]
        pairs = []
        if dx == 0:
            start = rows - 8 if dy > 0 else 0
            pairs.append((src.at[:, start : start + 8, :], rows_in.at[it, d]))
            pairs.append((row_out.at[it, d], row_in.at[it, d]))
        elif dy == 0:
            pairs.append((pack_out.at[it, d - 2], pack_in.at[it, d - 2]))
        else:
            start = rows - 16 if dy > 0 else 0
            pairs.append(
                (pack_out.at[it, 0 if dx > 0 else 1, start : start + 16], corner_in.at[it, d - 4])
            )
        if it == 0:
            pairs.append((own_tiss, near_tiss.at[d]))
        return [
            pltpu.make_async_remote_copy(
                src_ref=a,
                dst_ref=b,
                send_sem=halo_send.at[it, d, j],
                recv_sem=halo_recv.at[it, d, j],
                device_id={"gy": gy + dy, "gx": gx + dx},
                device_id_type=MESH,
            )
            for j, (a, b) in enumerate(pairs)
        ]

    def clear_missing(it):
        for d, (dy, dx) in enumerate(DIRS):

            @pl.when(jnp.logical_not(exists(-dy, -dx)))
            def _():
                if dx == 0:
                    rows_in[it, d] = jnp.zeros(rows_in.shape[2:], jnp.float32)
                    row_in[it, d] = jnp.zeros(row_in.shape[2:], jnp.float32)
                elif dy == 0:
                    pack_in[it, d - 2] = jnp.zeros(pack_in.shape[2:], jnp.float32)
                else:
                    corner_in[it, d - 4] = jnp.zeros(corner_in.shape[2:], jnp.float32)
                if it == 0:
                    near_tiss[d] = jnp.zeros(near_tiss.shape[1:], jnp.float32)

    def start_halo(src, it):
        for d, (dy, dx) in enumerate(DIRS):

            @pl.when(exists(dy, dx))
            def _():
                for copy in copies(src, it, d):
                    copy.start()

    def wait_halo(src, it):
        for d, (dy, dx) in enumerate(DIRS):

            @pl.when(exists(-dy, -dx))
            def _():
                for copy in copies(src, it, d):
                    copy.wait_recv()

    def wait_sent(src, it):
        for d, (dy, dx) in enumerate(DIRS):

            @pl.when(exists(dy, dx))
            def _():
                for copy in copies(src, it, d):
                    copy.wait_send()

    def sum_copy(k):
        flat = lax.rem(me + k, peers)
        return pltpu.make_async_remote_copy(
            src_ref=sums.at[0],
            dst_ref=sums.at[k],
            send_sem=sum_send.at[k],
            recv_sem=sum_recv.at[k],
            device_id={"gy": flat // nx, "gx": lax.rem(flat, nx)},
            device_id_type=MESH,
        )

    def spread_tissue():
        for zb in range(blocks_z):
            first = zb * blocks_y
            wide_tiss[zb, 1 : 1 + blocks_y, lanes : lanes + cols] = own_tiss[first : first + blocks_y]
            wide_tiss[zb, 1 : 1 + blocks_y, 0:lanes] = near_tiss[2, first : first + blocks_y, cols - lanes : cols]
            wide_tiss[zb, 1 : 1 + blocks_y, lanes + cols :] = near_tiss[3, first : first + blocks_y, 0:lanes]
            for row, source, at in ((0, (0, 4, 5), first + blocks_y - 1), (1 + blocks_y, (1, 6, 7), first)):
                mid_d, left_d, right_d = source
                wide_tiss[zb, row : row + 1, lanes : lanes + cols] = near_tiss[mid_d, at : at + 1, :]
                wide_tiss[zb, row : row + 1, 0:lanes] = near_tiss[left_d, at : at + 1, cols - lanes : cols]
                wide_tiss[zb, row : row + 1, lanes + cols :] = near_tiss[right_d, at : at + 1, 0:lanes]
            for ci, c in enumerate((-8, 0, 8)):
                moved = wide_tiss[zb, :, lanes + c : lanes + c + cols]
                for lt in range(tiles):
                    for rb in range(blocks_y + 2):
                        line = moved[rb : rb + 1, lt * lanes : (lt + 1) * lanes]
                        tissue[ci, lt, zb, rb * 8 : rb * 8 + 8] = jnp.broadcast_to(line, (8, lanes))

    def fill_centre(src):
        for z in range(depth):
            base[z, 9 : 9 + rows] = src[z]

    def fill_shifted(it):
        for z in range(depth):
            base[z, 0:1] = row_in[it, 0, z : z + 1]
            base[z, 1:9] = rows_in[it, 0, z]
            base[z, 9 + rows : 17 + rows] = rows_in[it, 1, z]
            base[z, 17 + rows : 18 + rows] = row_in[it, 1, z : z + 1]
        for side, (top, bottom) in enumerate(((0, 2), (1, 3))):
            edge[side, 0:9] = corner_in[it, top, 7:16]
            edge[side, 9 : 9 + rows] = pack_in[it, side]
            edge[side, 9 + rows : 18 + rows] = corner_in[it, bottom, 0:9]
        for z in range(depth):
            left = edge[0]
            if (112 - 16 * z) % lanes:
                left = pltpu.roll(left, (112 - 16 * z) % lanes, 1)
            right = edge[1]
            if z:
                right = pltpu.roll(right, (-16 * z) % lanes, 1)
            whole = jnp.concatenate([left, base[z], right], axis=1)
            for si, d in enumerate(SHIFTS):
                part = whole[:, lanes + d : lanes + d + cols]
                for lt in range(tiles):
                    shifted[si, lt, z] = part[:, lt * lanes : (lt + 1) * lanes]
        for ci in range(3):
            for lt in range(tiles):
                for z in range(depth):
                    vals = shifted[3 * ci + 1, lt, z, 1 : 17 + rows]
                    tissvals[ci, lt, z] = vals * tissue[ci, lt, z // 4]

    def smooth(src, dst, scale):
        numer[...] = jnp.zeros(numer.shape, jnp.float32)
        denom[...] = jnp.zeros(denom.shape, jnp.float32)
        span = rows + 8

        def body(step, carry):
            lt = step // 9
            bi = lax.rem(step // 3, 3)
            ci = lax.rem(step, 3)
            row = pl.multiple_of(bi * 8, 8)

            def squares(zi, a):
                inside, moved = 0 <= zi < depth, 0 <= zi + a < depth
                if not inside and not moved:
                    return None
                total = None
                for k in range(3):
                    if inside:
                        differ = shifted[3 + k, lt, zi, 8 : 8 + span]
                    if moved:
                        other = shifted[3 * ci + k, lt, zi + a, pl.ds(row, span)]
                        differ = differ - other if inside else other
                    part = differ * differ
                    total = part if total is None else total + part
                return total

            for a in (-4, 0, 4):
                low, high = max(0, -a), min(depth, depth - a)
                before, here = squares(low - 1, a), squares(low, a)
                pair = here if before is None else before + here
                for z in range(low, high):
                    after = squares(z + 1, a)
                    cube = pair if after is None else pair + after
                    distance = cube[0:rows] + cube[1 : rows + 1] + cube[2 : rows + 2]
                    weight = jnp.exp(distance * scale)
                    numer[lt, z] += weight * tissvals[ci, lt, z + a, pl.ds(row, rows)]
                    denom[lt, z] += weight * tissue[ci, lt, (z + a) // 4, pl.ds(row, rows)]
                    pair = here if after is None else here + after
                    here = after
            return carry

        lax.fori_loop(0, tiles * 9, body, 0)
        for lt in range(tiles):
            for z in range(depth):
                flag = tissue[1, lt, z // 4, 8 : 8 + rows]
                at = slice(lt * lanes, (lt + 1) * lanes)
                dst[z, :, at] = (
                    flag * numer[lt, z] / (denom[lt, z] + 1.0 - flag) + (1.0 - flag) * src[z, :, at]
                )

    spread = (
        lax.broadcasted_iota(jnp.int32, (blocks_x, cols), 1) // 8
        == lax.broadcasted_iota(jnp.int32, (blocks_x, cols), 0)
    ).astype(jnp.float32)
    for zb in range(blocks_z):
        flags = mask_ref[zb].astype(jnp.float32)
        own_tiss[zb * blocks_y : (zb + 1) * blocks_y] = jnp.dot(
            flags, spread, preferred_element_type=jnp.float32
        )
    total = jnp.zeros((8, cols), jnp.float32)
    count = jnp.zeros((8, cols), jnp.float32)
    for z in range(1, depth - 1):
        residual = vol_ref[z] - 0.5 * (vol_ref[z - 1] + vol_ref[z + 1])
        for yb in range(blocks_y):
            line = (z // 4) * blocks_y + yb
            flag = jnp.broadcast_to(own_tiss[line : line + 1], (8, cols))
            piece = residual[8 * yb : 8 * yb + 8]
            total = total + flag * piece * piece
            count = count + flag
    total = jnp.sum(total, axis=0, keepdims=True)
    count = jnp.sum(count, axis=0, keepdims=True)
    total = functools.reduce(jnp.add, [total[:, i * lanes : (i + 1) * lanes] for i in range(tiles)])
    count = functools.reduce(jnp.add, [count[:, i * lanes : (i + 1) * lanes] for i in range(tiles)])
    sums[0] = jnp.concatenate(
        [jnp.broadcast_to(total, (8, lanes)), jnp.broadcast_to(count, (8, lanes))], axis=0
    )
    make_packs(vol_ref, 0)
    pl.semaphore_wait(barrier, peers - 1)
    start_halo(vol_ref, 0)
    for k in range(1, peers):
        sum_copy(k).start()
    for it in range(ITERS):
        clear_missing(it)
    fill_centre(vol_ref)
    wait_halo(vol_ref, 0)
    spread_tissue()
    fill_shifted(0)
    for k in range(1, peers):
        sum_copy(k).wait_recv()
    everything = sums[0]
    for k in range(1, peers):
        everything = everything + sums[k]
    everything = jnp.sum(everything, axis=1, keepdims=True)
    summed = everything[0:1] * (2.0 / 3.0)
    tissue_count = everything[8:9]
    variance = summed / jnp.maximum(tissue_count, 1.0) + 1e-05
    width = 54.0 * smooth_ref[0] * smooth_ref[0]
    scale = jnp.broadcast_to(-1.0 / (width * variance), (rows, lanes))
    smooth(vol_ref, mid, scale)
    make_packs(mid, 1)
    start_halo(mid, 1)
    fill_centre(mid)
    wait_halo(mid, 1)
    fill_shifted(1)
    smooth(mid, out_ref, scale)
    wait_sent(vol_ref, 0)
    wait_sent(mid, 1)
    for k in range(1, peers):
        sum_copy(k).wait_send()


def on_device(volume, tissue_mask, smoothing):
    ny, nx = lax.axis_size("gy"), lax.axis_size("gx")
    depth, rows, cols = volume.shape
    blocks_z, blocks_y, blocks_x = tissue_mask.shape
    lanes = 128
    tiles = cols // lanes
    padded = -(-(rows + 18) // 8) * 8
    flag_rows = -(-(blocks_y + 2) // 8) * 8
    f32 = jnp.float32
    vmem = pl.BlockSpec(memory_space=pltpu.VMEM)
    return pl.pallas_call(
        functools.partial(kernel, ny, nx),
        out_shape=jax.ShapeDtypeStruct(volume.shape, f32),
        in_specs=[pl.BlockSpec(memory_space=pltpu.SMEM), vmem, vmem],
        out_specs=vmem,
        scratch_shapes=[
            pltpu.VMEM((depth, rows, cols), f32),
            pltpu.VMEM((depth, padded, cols), f32),
            pltpu.VMEM((len(SHIFTS), tiles, depth, padded, lanes), f32),
            pltpu.VMEM((3, tiles, blocks_z, rows + 16, lanes), f32),
            pltpu.VMEM((3, tiles, depth, rows + 16, lanes), f32),
            pltpu.VMEM((tiles, depth, rows, lanes), f32),
            pltpu.VMEM((tiles, depth, rows, lanes), f32),
            pltpu.VMEM((blocks_z * blocks_y, cols), f32),
            pltpu.VMEM((len(DIRS), blocks_z * blocks_y, cols), f32),
            pltpu.VMEM((blocks_z, flag_rows, cols + 2 * lanes), f32),
            pltpu.VMEM((ITERS, 2, depth, 8, cols), f32),
            pltpu.VMEM((ITERS, 2, depth, cols), f32),
            pltpu.VMEM((ITERS, 2, depth, cols), f32),
            pltpu.VMEM((ITERS, 2, rows, lanes), f32),
            pltpu.VMEM((ITERS, 2, rows, lanes), f32),
            pltpu.VMEM((ITERS, 4, 16, lanes), f32),
            pltpu.VMEM((2, padded, lanes), f32),
            pltpu.VMEM((ny * nx, 16, lanes), f32),
            pltpu.SemaphoreType.DMA((ny * nx,)),
            pltpu.SemaphoreType.DMA((ny * nx,)),
            pltpu.SemaphoreType.DMA((ITERS, len(DIRS), 3)),
            pltpu.SemaphoreType.DMA((ITERS, len(DIRS), 3)),
        ],
        compiler_params=pltpu.CompilerParams(collective_id=0, has_side_effects=True),
    )(smoothing, volume, tissue_mask)


def solution(mesh):
    placed = (P(None, ("slab", "gy"), "gx"), P(None, ("slab", "gy"), "gx"), P())
    return jax.shard_map(
        on_device,
        mesh=mesh,
        in_specs=placed,
        out_specs=P(None, ("slab", "gy"), "gx"),
        check_vma=False,
    )
```

time: 175 us -> 34.9 us (0.20)
  other arithmetic: 98 us -> 0 us
  blocking collectives: 34.1 us -> 0 us
  Pallas kernels: 0 us -> 32.4 us
  starting transfers between devices: 14.3 us -> 0 us
  waiting for transfers between devices: 11.7 us -> 0 us
  local copies, waits for them, and re-layouts: 12.2 us -> 1.67 us
  between operations: 3.22 us -> 0.66 us
    add x97 -> x0, other arithmetic: 85.5 us -> none  [the longest x54 45.3 us: box_sum(): second = first[:, 0:rows] + first[:, 1:rows + 1] + first[:, 2:rows + 2]]
    psum x1 -> x0, blocking collectives: 34.1 us -> none  [on_device(): summed, tissue_count = lax.psum((local_sum, local_count), ('gy', 'gx'))]
    pallas_call x0 -> x1, Pallas kernels: none -> 32.4 us  [on_device(): pl.pallas_call(functools.partial(kernel, ny, nx), out_shape=jax.ShapeDtyp...]
    ppermute x8 -> x0, starting transfers between devices: 14.3 us -> none  [the longest x4 8.89 us: extended(): lax.ppermute(lax.slice_in_dim(block, block.shape[dim] - width, None, axis...]
    ppermute x8 -> x0, waiting for transfers between devices: 11.7 us -> none  [the longest x4 10.3 us: extended(): lax.ppermute(lax.slice_in_dim(block, 0, width, axis=dim), axis, backward)]
    convert_element_type x2 -> x0, local copies, waits for them, and re-layouts: 8.09 us -> none  [expand_mask(): spread.reshape(blocks_z * 4, blocks_y * 8, blocks_x * 8).astype(jnp.float32)]
    mul x6 -> x0, other arithmetic: 6.78 us -> none  [smooth_once(): distance = box_sum(differ * differ, depth, rows, cols)]
    concatenate x5 -> x0, other arithmetic: 4.35 us -> none  [extended(): block = jnp.concatenate([low, block, high], axis=dim)]
  transfers between devices with their start and end apart: 8 -> 0, of which waited for: 5 -> 0; matrix products, arithmetic and copies ran while one was open for 3% -> 0% of each run, Pallas kernels for 0% -> 0%
where the time goes in v1:
time: 34.9 us; the launch traced here: 34.8 us
  Pallas kernels  32.4 us (93%)
  local copies, waits for them, and re-layouts  1.67 us (5%)
  between operations  0.66 us (2%)
    pallas_call x1, Pallas kernels, on_device(): pl.pallas_call(functools.partial(kernel, ny, nx), out_shape=jax.ShapeDtyp...  32.4 us
    unnamed x1, local copies, waits for them, and re-layouts  1.67 us

profile of v1, /device:TPU:0, one launch (start us, length us, event | category | flops | bytes accessed | tf_op | source)
XLA Modules:
  0.0 34.8 jit_solution(16459409591305975697)
XLA Ops:
  0.7 32.4 %shard_map.37 = f32[8,32,256]{2,1,0:T(8,128)} custom-call(f32[1]{0:T(128)S(6)} %copy.5.smooth_ref, f32[8,32,256]{2,1,0:T(8,128)} %vol_ref.1, s32[2,4,32]{2,1,0:T(4,128)} %mask_ref.1), custom_call_target="tpu_custom_call" | custom-call | tf_op jit(solution)/shard_map/pallas_call | solution.py:315
  33.1 1.7 %copy.6 = f32[8,32,256]{2,1,0:T(8,128)} copy(f32[8,32,256]{2,1,0:T(8,128)} %shard_map.37) | data formatting | bytes 524288

commit v2 on v1

--- a/solution.py
+++ b/solution.py
@@ -9,15 +9,16 @@
 
 MESH = pl.DeviceIdType.MESH
 ITERS = 2
+LOG2E = 1.4426950408889634
 SHIFTS = (-9, -8, -7, -1, 0, 1, 7, 8, 9)
 DIRS = ((1, 0), (-1, 0), (0, 1), (0, -1), (1, 1), (1, -1), (-1, 1), (-1, -1))
 
 
 def kernel(
-    ny, nx, smooth_ref, vol_ref, mask_ref, out_ref,
+    ny, nx, smooth_ref, vol_hbm, mask_hbm, out_ref, vol_ref, mask_ref, cubes,
     mid, base, shifted, tissue, tissvals, numer, denom, own_tiss, near_tiss, wide_tiss,
     rows_in, row_in, row_out, pack_out, pack_in, corner_in, edge, sums,
-    sum_send, sum_recv, halo_send, halo_recv,
+    load_sem, sum_send, sum_recv, halo_send, halo_recv,
 ):
     depth, rows, cols = vol_ref.shape
     lanes = 128
@@ -34,6 +35,13 @@
         pl.semaphore_signal(
             barrier, inc=1, device_id={"gy": flat // nx, "gx": lax.rem(flat, nx)}, device_id_type=MESH
         )
+
+    loads = [
+        pltpu.make_async_copy(mask_hbm, mask_ref, load_sem.at[0]),
+        pltpu.make_async_copy(vol_hbm, vol_ref, load_sem.at[1]),
+    ]
+    for load in loads:
+        load.start()
 
     def exists(dy, dx):
         found = None
@@ -217,6 +225,7 @@
                     total = part if total is None else total + part
                 return total
 
+            slot = 0
             for a in (-4, 0, 4):
                 low, high = max(0, -a), min(depth, depth - a)
                 before, here = squares(low - 1, a), squares(low, a)
@@ -224,8 +233,10 @@
                 for z in range(low, high):
                     after = squares(z + 1, a)
                     cube = pair if after is None else pair + after
-                    distance = cube[0:rows] + cube[1 : rows + 1] + cube[2 : rows + 2]
-                    weight = jnp.exp(distance * scale)
+                    cubes[slot] = cube
+                    distance = cube[0:rows] + cubes[slot, 1 : rows + 1] + cubes[slot, 2 : rows + 2]
+                    slot += 1
+                    weight = jnp.exp2(distance * scale)
                     numer[lt, z] += weight * tissvals[ci, lt, z + a, pl.ds(row, rows)]
                     denom[lt, z] += weight * tissue[ci, lt, (z + a) // 4, pl.ds(row, rows)]
                     pair = here if after is None else here + after
@@ -241,6 +252,7 @@
                     flag * numer[lt, z] / (denom[lt, z] + 1.0 - flag) + (1.0 - flag) * src[z, :, at]
                 )
 
+    loads[0].wait()
     spread = (
         lax.broadcasted_iota(jnp.int32, (blocks_x, cols), 1) // 8
         == lax.broadcasted_iota(jnp.int32, (blocks_x, cols), 0)
@@ -250,6 +262,7 @@
         own_tiss[zb * blocks_y : (zb + 1) * blocks_y] = jnp.dot(
             flags, spread, preferred_element_type=jnp.float32
         )
+    loads[1].wait()
     total = jnp.zeros((8, cols), jnp.float32)
     count = jnp.zeros((8, cols), jnp.float32)
     for z in range(1, depth - 1):
@@ -264,14 +277,15 @@
     count = jnp.sum(count, axis=0, keepdims=True)
     total = functools.reduce(jnp.add, [total[:, i * lanes : (i + 1) * lanes] for i in range(tiles)])
     count = functools.reduce(jnp.add, [count[:, i * lanes : (i + 1) * lanes] for i in range(tiles)])
-    sums[0] = jnp.concatenate(
-        [jnp.broadcast_to(total, (8, lanes)), jnp.broadcast_to(count, (8, lanes))], axis=0
+    line = lax.broadcasted_iota(jnp.int32, (8, lanes), 0)
+    sums[0] = jnp.where(
+        line < 4, jnp.broadcast_to(total, (8, lanes)), jnp.broadcast_to(count, (8, lanes))
     )
     make_packs(vol_ref, 0)
     pl.semaphore_wait(barrier, peers - 1)
+    for k in range(1, peers):
+        sum_copy(k).start()
     start_halo(vol_ref, 0)
-    for k in range(1, peers):
-        sum_copy(k).start()
     for it in range(ITERS):
         clear_missing(it)
     fill_centre(vol_ref)
@@ -285,10 +299,10 @@
         everything = everything + sums[k]
     everything = jnp.sum(everything, axis=1, keepdims=True)
     summed = everything[0:1] * (2.0 / 3.0)
-    tissue_count = everything[8:9]
+    tissue_count = everything[4:5]
     variance = summed / jnp.maximum(tissue_count, 1.0) + 1e-05
     width = 54.0 * smooth_ref[0] * smooth_ref[0]
-    scale = jnp.broadcast_to(-1.0 / (width * variance), (rows, lanes))
+    scale = jnp.broadcast_to(-LOG2E / (width * variance), (rows, lanes))
     smooth(vol_ref, mid, scale)
     make_packs(mid, 1)
     start_halo(mid, 1)
@@ -312,12 +326,16 @@
     flag_rows = -(-(blocks_y + 2) // 8) * 8
     f32 = jnp.float32
     vmem = pl.BlockSpec(memory_space=pltpu.VMEM)
+    anywhere = pl.BlockSpec(memory_space=pltpu.HBM)
     return pl.pallas_call(
         functools.partial(kernel, ny, nx),
         out_shape=jax.ShapeDtypeStruct(volume.shape, f32),
-        in_specs=[pl.BlockSpec(memory_space=pltpu.SMEM), vmem, vmem],
+        in_specs=[pl.BlockSpec(memory_space=pltpu.SMEM), anywhere, anywhere],
         out_specs=vmem,
         scratch_shapes=[
+            pltpu.VMEM((depth, rows, cols), f32),
+            pltpu.VMEM((blocks_z, blocks_y, blocks_x), jnp.int32),
+            pltpu.VMEM((20, rows + 8, lanes), f32),
             pltpu.VMEM((depth, rows, cols), f32),
             pltpu.VMEM((depth, padded, cols), f32),
             pltpu.VMEM((len(SHIFTS), tiles, depth, padded, lanes), f32),
@@ -335,13 +353,16 @@
             pltpu.VMEM((ITERS, 2, rows, lanes), f32),
             pltpu.VMEM((ITERS, 4, 16, lanes), f32),
             pltpu.VMEM((2, padded, lanes), f32),
-            pltpu.VMEM((ny * nx, 16, lanes), f32),
+            pltpu.VMEM((ny * nx, 8, lanes), f32),
+            pltpu.SemaphoreType.DMA((2,)),
             pltpu.SemaphoreType.DMA((ny * nx,)),
             pltpu.SemaphoreType.DMA((ny * nx,)),
             pltpu.SemaphoreType.DMA((ITERS, len(DIRS), 3)),
             pltpu.SemaphoreType.DMA((ITERS, len(DIRS), 3)),
         ],
-        compiler_params=pltpu.CompilerParams(collective_id=0, has_side_effects=True),
+        compiler_params=pltpu.CompilerParams(
+            collective_id=0, has_side_effects=True, vmem_limit_bytes=16 * 2**20
+        ),
     )(smoothing, volume, tissue_mask)
 
 

time: 34.9 us -> 34.1 us (0.977)
  Pallas kernels: 32.4 us -> 30.9 us
  local copies, waits for them, and re-layouts: 1.67 us -> 2.33 us
    pallas_call x1, Pallas kernels: 32.4 us -> 30.9 us  [on_device(): pl.pallas_call(functools.partial(kernel, ny, nx), out_shape=jax.ShapeDtyp...]
    unnamed x1 -> x5, local copies, waits for them, and re-layouts: 1.67 us -> 2.33 us
where the time goes in v2:
time: 34.1 us; the launch traced here: 34 us
  Pallas kernels  30.9 us (91%)
  local copies, waits for them, and re-layouts  2.33 us (7%)
  between operations  0.67 us (2%)
    pallas_call x1, Pallas kernels, on_device(): pl.pallas_call(functools.partial(kernel, ny, nx), out_shape=jax.ShapeDtyp...  30.9 us
    unnamed x5, local copies, waits for them, and re-layouts  2.33 us

profile of v2, /device:TPU:0, one launch (start us, length us, event | category | flops | bytes accessed | tf_op | source)
XLA Modules:
  0.0 34.0 jit_solution(10558321984028302332)
XLA Ops:
  0.7 0.0 copy-start
  0.7 0.9 %copy-done = f32[8,32,256]{2,1,0:T(8,128)S(1)} copy-done((f32[8,32,256]{2,1,0:T(8,128)S(1)}, f32[8,32,256]{2,1,0:T(8,128)}, u32[]{:S(2)}) %copy-start) | copy-done | bytes 262168
  1.6 0.0 copy-start.1
  1.6 0.7 %copy-done.1 = s32[2,4,32]{2,1,0:T(4,128)S(1)} copy-done((s32[2,4,32]{2,1,0:T(4,128)S(1)}, s32[2,4,32]{2,1,0:T(4,128)}, u32[]{:S(2)}) %copy-start.1) | copy-done | bytes 1048
  2.3 30.9 %shard_map.37 = f32[8,32,256]{2,1,0:T(8,128)S(1)} custom-call(f32[1]{0:T(128)S(6)} %copy.5.smooth_ref, f32[8,32,256]{2,1,0:T(8,128)S(1)} %copy-done, s32[2,4,32]{2,1,0:T(4,128)S(1)} %copy-done.1), custom_call_target="tpu_custom_call" | custom-call | tf_op jit(solution)/shard_map/pallas_call | solution.py:330
  33.2 0.7 %copy.6 = f32[8,32,256]{2,1,0:T(8,128)} copy(f32[8,32,256]{2,1,0:T(8,128)S(1)} %shard_map.37) | data formatting | bytes 524288
Async XLA Ops:
  0.7 1.0 %copy-start = (f32[8,32,256]{2,1,0:T(8,128)S(1)}, f32[8,32,256]{2,1,0:T(8,128)}, u32[]{:S(2)}) copy-start(f32[8,32,256]{2,1,0:T(8,128)} %vol_hbm.1) | copy-start | bytes 786436
  1.6 0.7 %copy-start.1 = (s32[2,4,32]{2,1,0:T(4,128)S(1)}, s32[2,4,32]{2,1,0:T(4,128)}, u32[]{:S(2)}) copy-start(s32[2,4,32]{2,1,0:T(4,128)} %mask_hbm.1) | copy-start | bytes 3076

commit v3 on v2

--- a/solution.py
+++ b/solution.py
@@ -8,7 +8,7 @@
 from jax.sharding import PartitionSpec as P
 
 MESH = pl.DeviceIdType.MESH
-ITERS = 2
+PHASES = ((0, 2), (0, 1), (1, 2))
 LOG2E = 1.4426950408889634
 SHIFTS = (-9, -8, -7, -1, 0, 1, 7, 8, 9)
 DIRS = ((1, 0), (-1, 0), (0, 1), (0, -1), (1, 1), (1, -1), (-1, 1), (-1, -1))
@@ -26,6 +26,8 @@
     blocks_z, blocks_y, blocks_x = mask_ref.shape
     padded = shifted.shape[3]
     peers = ny * nx
+    half = depth // 2
+    phases = [(low * half, high * half) for low, high in PHASES]
     gy, gx = lax.axis_index("gy"), lax.axis_index("gx")
     me = gy * nx + gx
 
@@ -59,7 +61,7 @@
         group = lane_group((rows, lanes))
         right = jnp.zeros((rows, lanes), jnp.float32)
         left = right
-        for z in range(depth):
+        for z in range(*phases[it]):
             high = pltpu.roll(src[z, :, cols - lanes : cols], (16 * z + 16) % lanes, 1)
             right = jnp.where(group == z, high, right)
             low = src[z, :, 0:lanes]
@@ -76,7 +78,8 @@
         pairs = []
         if dx == 0:
             start = rows - 8 if dy > 0 else 0
-            pairs.append((src.at[:, start : start + 8, :], rows_in.at[it, d]))
+            low, high = phases[it]
+            pairs.append((src.at[low:high, start : start + 8, :], rows_in.at[it, d, low:high]))
             pairs.append((row_out.at[it, d], row_in.at[it, d]))
         elif dy == 0:
             pairs.append((pack_out.at[it, d - 2], pack_in.at[it, d - 2]))
@@ -167,12 +170,12 @@
                         line = moved[rb : rb + 1, lt * lanes : (lt + 1) * lanes]
                         tissue[ci, lt, zb, rb * 8 : rb * 8 + 8] = jnp.broadcast_to(line, (8, lanes))
 
-    def fill_centre(src):
-        for z in range(depth):
+    def fill_centre(src, it):
+        for z in range(*phases[it]):
             base[z, 9 : 9 + rows] = src[z]
 
     def fill_shifted(it):
-        for z in range(depth):
+        for z in range(*phases[it]):
             base[z, 0:1] = row_in[it, 0, z : z + 1]
             base[z, 1:9] = rows_in[it, 0, z]
             base[z, 9 + rows : 17 + rows] = rows_in[it, 1, z]
@@ -181,7 +184,7 @@
             edge[side, 0:9] = corner_in[it, top, 7:16]
             edge[side, 9 : 9 + rows] = pack_in[it, side]
             edge[side, 9 + rows : 18 + rows] = corner_in[it, bottom, 0:9]
-        for z in range(depth):
+        for z in range(*phases[it]):
             left = edge[0]
             if (112 - 16 * z) % lanes:
                 left = pltpu.roll(left, (112 - 16 * z) % lanes, 1)
@@ -195,13 +198,15 @@
                     shifted[si, lt, z] = part[:, lt * lanes : (lt + 1) * lanes]
         for ci in range(3):
             for lt in range(tiles):
-                for z in range(depth):
+                for z in range(*phases[it]):
                     vals = shifted[3 * ci + 1, lt, z, 1 : 17 + rows]
                     tissvals[ci, lt, z] = vals * tissue[ci, lt, z // 4]
 
-    def smooth(src, dst, scale):
+    def clear_sums():
         numer[...] = jnp.zeros(numer.shape, jnp.float32)
         denom[...] = jnp.zeros(denom.shape, jnp.float32)
+
+    def gather(passes, scale):
         span = rows + 8
 
         def body(step, carry):
@@ -226,8 +231,7 @@
                 return total
 
             slot = 0
-            for a in (-4, 0, 4):
-                low, high = max(0, -a), min(depth, depth - a)
+            for a, low, high in passes:
                 before, here = squares(low - 1, a), squares(low, a)
                 pair = here if before is None else before + here
                 for z in range(low, high):
@@ -244,8 +248,10 @@
             return carry
 
         lax.fori_loop(0, tiles * 9, body, 0)
+
+    def finish(src, dst, low, high):
         for lt in range(tiles):
-            for z in range(depth):
+            for z in range(low, high):
                 flag = tissue[1, lt, z // 4, 8 : 8 + rows]
                 at = slice(lt * lanes, (lt + 1) * lanes)
                 dst[z, :, at] = (
@@ -286,9 +292,10 @@
     for k in range(1, peers):
         sum_copy(k).start()
     start_halo(vol_ref, 0)
-    for it in range(ITERS):
+    for it in range(len(PHASES)):
         clear_missing(it)
-    fill_centre(vol_ref)
+    fill_centre(vol_ref, 0)
+    clear_sums()
     wait_halo(vol_ref, 0)
     spread_tissue()
     fill_shifted(0)
@@ -303,15 +310,24 @@
     variance = summed / jnp.maximum(tissue_count, 1.0) + 1e-05
     width = 54.0 * smooth_ref[0] * smooth_ref[0]
     scale = jnp.broadcast_to(-LOG2E / (width * variance), (rows, lanes))
-    smooth(vol_ref, mid, scale)
-    make_packs(mid, 1)
-    start_halo(mid, 1)
-    fill_centre(mid)
+    for it, passes in ((1, ((0, 0, half), (4, 0, half))), (2, ((0, half, depth), (-4, half, depth)))):
+        gather(passes, scale)
+        finish(vol_ref, mid, *phases[it])
+        make_packs(mid, it)
+        start_halo(mid, it)
+    clear_sums()
+    fill_centre(mid, 1)
     wait_halo(mid, 1)
     fill_shifted(1)
-    smooth(mid, out_ref, scale)
+    gather(((0, 0, half - 1),), scale)
+    fill_centre(mid, 2)
+    wait_halo(mid, 2)
+    fill_shifted(2)
+    gather(((0, half - 1, depth), (4, 0, half), (-4, half, depth)), scale)
+    finish(mid, out_ref, 0, depth)
     wait_sent(vol_ref, 0)
     wait_sent(mid, 1)
+    wait_sent(mid, 2)
     for k in range(1, peers):
         sum_copy(k).wait_send()
 
@@ -346,19 +362,19 @@
             pltpu.VMEM((blocks_z * blocks_y, cols), f32),
             pltpu.VMEM((len(DIRS), blocks_z * blocks_y, cols), f32),
             pltpu.VMEM((blocks_z, flag_rows, cols + 2 * lanes), f32),
-            pltpu.VMEM((ITERS, 2, depth, 8, cols), f32),
-            pltpu.VMEM((ITERS, 2, depth, cols), f32),
-            pltpu.VMEM((ITERS, 2, depth, cols), f32),
-            pltpu.VMEM((ITERS, 2, rows, lanes), f32),
-            pltpu.VMEM((ITERS, 2, rows, lanes), f32),
-            pltpu.VMEM((ITERS, 4, 16, lanes), f32),
+            pltpu.VMEM((len(PHASES), 2, depth, 8, cols), f32),
+            pltpu.VMEM((len(PHASES), 2, depth, cols), f32),
+            pltpu.VMEM((len(PHASES), 2, depth, cols), f32),
+            pltpu.VMEM((len(PHASES), 2, rows, lanes), f32),
+            pltpu.VMEM((len(PHASES), 2, rows, lanes), f32),
+            pltpu.VMEM((len(PHASES), 4, 16, lanes), f32),
             pltpu.VMEM((2, padded, lanes), f32),
             pltpu.VMEM((ny * nx, 8, lanes), f32),
             pltpu.SemaphoreType.DMA((2,)),
             pltpu.SemaphoreType.DMA((ny * nx,)),
             pltpu.SemaphoreType.DMA((ny * nx,)),
-            pltpu.SemaphoreType.DMA((ITERS, len(DIRS), 3)),
-            pltpu.SemaphoreType.DMA((ITERS, len(DIRS), 3)),
+            pltpu.SemaphoreType.DMA((len(PHASES), len(DIRS), 3)),
+            pltpu.SemaphoreType.DMA((len(PHASES), len(DIRS), 3)),
         ],
         compiler_params=pltpu.CompilerParams(
             collective_id=0, has_side_effects=True, vmem_limit_bytes=16 * 2**20

time: 34.1 us -> 33.1 us (0.971)
  Pallas kernels: 30.9 us -> 29.9 us
    pallas_call x1, Pallas kernels: 30.9 us -> 29.9 us  [on_device(): pl.pallas_call(functools.partial(kernel, ny, nx), out_shape=jax.ShapeDtyp...]
where the time goes in v3:
time: 33.1 us; the launch traced here: 32.9 us
  Pallas kernels  29.9 us (90%)
  local copies, waits for them, and re-layouts  2.33 us (7%)
  between operations  0.67 us (2%)
    pallas_call x1, Pallas kernels, on_device(): pl.pallas_call(functools.partial(kernel, ny, nx), out_shape=jax.ShapeDtyp...  29.9 us
    unnamed x5, local copies, waits for them, and re-layouts  2.33 us

profile of v3, /device:TPU:0, one launch (start us, length us, event | category | flops | bytes accessed | tf_op | source)
XLA Modules:
  0.0 32.9 jit_solution(13994556183362682836)
XLA Ops:
  0.7 0.0 copy-start
  0.7 0.9 %copy-done = f32[8,32,256]{2,1,0:T(8,128)S(1)} copy-done((f32[8,32,256]{2,1,0:T(8,128)S(1)}, f32[8,32,256]{2,1,0:T(8,128)}, u32[]{:S(2)}) %copy-start) | copy-done | bytes 262168
  1.6 0.0 copy-start.1
  1.6 0.7 %copy-done.1 = s32[2,4,32]{2,1,0:T(4,128)S(1)} copy-done((s32[2,4,32]{2,1,0:T(4,128)S(1)}, s32[2,4,32]{2,1,0:T(4,128)}, u32[]{:S(2)}) %copy-start.1) | copy-done | bytes 1048
  2.3 29.9 %shard_map.37 = f32[8,32,256]{2,1,0:T(8,128)S(1)} custom-call(f32[1]{0:T(128)S(6)} %copy.5.smooth_ref, f32[8,32,256]{2,1,0:T(8,128)S(1)} %copy-done, s32[2,4,32]{2,1,0:T(4,128)S(1)} %copy-done.1), custom_call_target="tpu_custom_call" | custom-call | tf_op jit(solution)/shard_map/pallas_call | solution.py:346
  32.2 0.7 %copy.6 = f32[8,32,256]{2,1,0:T(8,128)} copy(f32[8,32,256]{2,1,0:T(8,128)S(1)} %shard_map.37) | data formatting | bytes 524288
Async XLA Ops:
  0.7 1.0 %copy-start = (f32[8,32,256]{2,1,0:T(8,128)S(1)}, f32[8,32,256]{2,1,0:T(8,128)}, u32[]{:S(2)}) copy-start(f32[8,32,256]{2,1,0:T(8,128)} %vol_hbm.1) | copy-start | bytes 786436
  1.6 0.7 %copy-start.1 = (s32[2,4,32]{2,1,0:T(4,128)S(1)}, s32[2,4,32]{2,1,0:T(4,128)}, u32[]{:S(2)}) copy-start(s32[2,4,32]{2,1,0:T(4,128)} %mask_hbm.1) | copy-start | bytes 3076

commit v4 on v3

--- a/solution.py
+++ b/solution.py
@@ -89,7 +89,8 @@
                 (pack_out.at[it, 0 if dx > 0 else 1, start : start + 16], corner_in.at[it, d - 4])
             )
         if it == 0:
-            pairs.append((own_tiss, near_tiss.at[d]))
+            at = {1: slice(cols - lanes, cols), -1: slice(0, lanes), 0: slice(0, cols)}[dx]
+            pairs.append((own_tiss.at[:, at], near_tiss.at[d, :, at]))
         return [
             pltpu.make_async_remote_copy(
                 src_ref=a,
@@ -283,9 +284,11 @@
     count = jnp.sum(count, axis=0, keepdims=True)
     total = functools.reduce(jnp.add, [total[:, i * lanes : (i + 1) * lanes] for i in range(tiles)])
     count = functools.reduce(jnp.add, [count[:, i * lanes : (i + 1) * lanes] for i in range(tiles)])
-    line = lax.broadcasted_iota(jnp.int32, (8, lanes), 0)
+    lane = lax.broadcasted_iota(jnp.int32, (1, lanes), 1)
     sums[0] = jnp.where(
-        line < 4, jnp.broadcast_to(total, (8, lanes)), jnp.broadcast_to(count, (8, lanes))
+        lane < lanes // 2,
+        jnp.sum(total, axis=1, keepdims=True),
+        jnp.sum(count, axis=1, keepdims=True),
     )
     make_packs(vol_ref, 0)
     pl.semaphore_wait(barrier, peers - 1)
@@ -304,9 +307,8 @@
     everything = sums[0]
     for k in range(1, peers):
         everything = everything + sums[k]
-    everything = jnp.sum(everything, axis=1, keepdims=True)
-    summed = everything[0:1] * (2.0 / 3.0)
-    tissue_count = everything[4:5]
+    summed = everything[:, 0:1] * (2.0 / 3.0)
+    tissue_count = everything[:, lanes // 2 : lanes // 2 + 1]
     variance = summed / jnp.maximum(tissue_count, 1.0) + 1e-05
     width = 54.0 * smooth_ref[0] * smooth_ref[0]
     scale = jnp.broadcast_to(-LOG2E / (width * variance), (rows, lanes))
@@ -369,7 +371,7 @@
             pltpu.VMEM((len(PHASES), 2, rows, lanes), f32),
             pltpu.VMEM((len(PHASES), 4, 16, lanes), f32),
             pltpu.VMEM((2, padded, lanes), f32),
-            pltpu.VMEM((ny * nx, 8, lanes), f32),
+            pltpu.VMEM((ny * nx, 1, lanes), f32),
             pltpu.SemaphoreType.DMA((2,)),
             pltpu.SemaphoreType.DMA((ny * nx,)),
             pltpu.SemaphoreType.DMA((ny * nx,)),

time: 33.1 us -> 32.1 us (0.970)
  Pallas kernels: 29.9 us -> 28.9 us
    pallas_call x1, Pallas kernels: 29.9 us -> 28.9 us  [on_device(): pl.pallas_call(functools.partial(kernel, ny, nx), out_shape=jax.ShapeDtyp...]
where the time goes in v4:
time: 32.1 us; the launch traced here: 31.9 us
  Pallas kernels  28.9 us (90%)
  local copies, waits for them, and re-layouts  2.33 us (7%)
  between operations  0.67 us (2%)
    pallas_call x1, Pallas kernels, on_device(): pl.pallas_call(functools.partial(kernel, ny, nx), out_shape=jax.ShapeDtyp...  28.9 us
    unnamed x5, local copies, waits for them, and re-layouts  2.33 us

profile of v4, /device:TPU:0, one launch (start us, length us, event | category | flops | bytes accessed | tf_op | source)
XLA Modules:
  0.0 31.9 jit_solution(12851313549635316734)
XLA Ops:
  0.7 0.0 copy-start
  0.7 0.9 %copy-done = f32[8,32,256]{2,1,0:T(8,128)S(1)} copy-done((f32[8,32,256]{2,1,0:T(8,128)S(1)}, f32[8,32,256]{2,1,0:T(8,128)}, u32[]{:S(2)}) %copy-start) | copy-done | bytes 262168
  1.6 0.0 copy-start.1
  1.6 0.7 %copy-done.1 = s32[2,4,32]{2,1,0:T(4,128)S(1)} copy-done((s32[2,4,32]{2,1,0:T(4,128)S(1)}, s32[2,4,32]{2,1,0:T(4,128)}, u32[]{:S(2)}) %copy-start.1) | copy-done | bytes 1048
  2.3 28.9 %shard_map.37 = f32[8,32,256]{2,1,0:T(8,128)S(1)} custom-call(f32[1]{0:T(128)S(6)} %copy.5.smooth_ref, f32[8,32,256]{2,1,0:T(8,128)S(1)} %copy-done, s32[2,4,32]{2,1,0:T(4,128)S(1)} %copy-done.1), custom_call_target="tpu_custom_call" | custom-call | tf_op jit(solution)/shard_map/pallas_call | solution.py:348
  31.2 0.7 %copy.6 = f32[8,32,256]{2,1,0:T(8,128)} copy(f32[8,32,256]{2,1,0:T(8,128)S(1)} %shard_map.37) | data formatting | bytes 524288
Async XLA Ops:
  0.7 1.0 %copy-start = (f32[8,32,256]{2,1,0:T(8,128)S(1)}, f32[8,32,256]{2,1,0:T(8,128)}, u32[]{:S(2)}) copy-start(f32[8,32,256]{2,1,0:T(8,128)} %vol_hbm.1) | copy-start | bytes 786436
  1.6 0.7 %copy-start.1 = (s32[2,4,32]{2,1,0:T(4,128)S(1)}, s32[2,4,32]{2,1,0:T(4,128)}, u32[]{:S(2)}) copy-start(s32[2,4,32]{2,1,0:T(4,128)} %mask_hbm.1) | copy-start | bytes 3076

commit v5 on v4

--- a/solution.py
+++ b/solution.py
@@ -381,7 +381,11 @@
         compiler_params=pltpu.CompilerParams(
             collective_id=0, has_side_effects=True, vmem_limit_bytes=16 * 2**20
         ),
-    )(smoothing, volume, tissue_mask)
+    )(
+        smoothing,
+        pltpu.with_memory_space_constraint(volume, pltpu.HBM),
+        pltpu.with_memory_space_constraint(tissue_mask, pltpu.HBM),
+    )
 
 
 def solution(mesh):

time: 32.1 us -> 30.5 us (0.950)
  local copies, waits for them, and re-layouts: 2.33 us -> 0.71 us
    unnamed x5 -> x1, local copies, waits for them, and re-layouts: 2.33 us -> 0.71 us
where the time goes in v5:
time: 30.5 us; the launch traced here: 30.3 us
  Pallas kernels  29 us (95%)
  local copies, waits for them, and re-layouts  0.71 us (2%)
  between operations  0.66 us (2%)
    pallas_call x1, Pallas kernels, on_device(): pl.pallas_call(functools.partial(kernel, ny, nx), out_shape=jax.ShapeDtyp...  29 us
    unnamed x1, local copies, waits for them, and re-layouts  0.71 us

profile of v5, /device:TPU:0, one launch (start us, length us, event | category | flops | bytes accessed | tf_op | source)
XLA Modules:
  0.0 30.3 jit_solution(12044282309982546981)
XLA Ops:
  0.7 29.0 %shard_map.37 = f32[8,32,256]{2,1,0:T(8,128)S(1)} custom-call(f32[1]{0:T(128)S(6)} %copy.5.smooth_ref, f32[8,32,256]{2,1,0:T(8,128)} %vol_hbm.1, s32[2,4,32]{2,1,0:T(4,128)} %mask_hbm.1), custom_call_target="tpu_custom_call" | custom-call | tf_op jit(solution)/shard_map/pallas_call | solution.py:348
  29.6 0.7 %copy.6 = f32[8,32,256]{2,1,0:T(8,128)} copy(f32[8,32,256]{2,1,0:T(8,128)S(1)} %shard_map.37) | data formatting | bytes 524288

commit v6 on v5

--- a/solution.py
+++ b/solution.py
@@ -211,12 +211,11 @@
         span = rows + 8
 
         def body(step, carry):
-            lt = step // 9
-            bi = lax.rem(step // 3, 3)
-            ci = lax.rem(step, 3)
+            lt = step // 3
+            bi = lax.rem(step, 3)
             row = pl.multiple_of(bi * 8, 8)
 
-            def squares(zi, a):
+            def squares(zi, a, ci):
                 inside, moved = 0 <= zi < depth, 0 <= zi + a < depth
                 if not inside and not moved:
                     return None
@@ -232,23 +231,24 @@
                 return total
 
             slot = 0
-            for a, low, high in passes:
-                before, here = squares(low - 1, a), squares(low, a)
-                pair = here if before is None else before + here
-                for z in range(low, high):
-                    after = squares(z + 1, a)
-                    cube = pair if after is None else pair + after
-                    cubes[slot] = cube
-                    distance = cube[0:rows] + cubes[slot, 1 : rows + 1] + cubes[slot, 2 : rows + 2]
-                    slot += 1
-                    weight = jnp.exp2(distance * scale)
-                    numer[lt, z] += weight * tissvals[ci, lt, z + a, pl.ds(row, rows)]
-                    denom[lt, z] += weight * tissue[ci, lt, (z + a) // 4, pl.ds(row, rows)]
-                    pair = here if after is None else here + after
-                    here = after
+            for ci in range(3):
+                for a, low, high in passes:
+                    before, here = squares(low - 1, a, ci), squares(low, a, ci)
+                    pair = here if before is None else before + here
+                    for z in range(low, high):
+                        after = squares(z + 1, a, ci)
+                        cube = pair if after is None else pair + after
+                        cubes[slot] = cube
+                        distance = cube[0:rows] + cubes[slot, 1 : rows + 1] + cubes[slot, 2 : rows + 2]
+                        slot += 1
+                        weight = jnp.exp2(distance * scale)
+                        numer[lt, z] += weight * tissvals[ci, lt, z + a, pl.ds(row, rows)]
+                        denom[lt, z] += weight * tissue[ci, lt, (z + a) // 4, pl.ds(row, rows)]
+                        pair = here if after is None else here + after
+                        here = after
             return carry
 
-        lax.fori_loop(0, tiles * 9, body, 0)
+        lax.fori_loop(0, tiles * 3, body, 0)
 
     def finish(src, dst, low, high):
         for lt in range(tiles):
@@ -353,7 +353,7 @@
         scratch_shapes=[
             pltpu.VMEM((depth, rows, cols), f32),
             pltpu.VMEM((blocks_z, blocks_y, blocks_x), jnp.int32),
-            pltpu.VMEM((20, rows + 8, lanes), f32),
+            pltpu.VMEM((60, rows + 8, lanes), f32),
             pltpu.VMEM((depth, rows, cols), f32),
             pltpu.VMEM((depth, padded, cols), f32),
             pltpu.VMEM((len(SHIFTS), tiles, depth, padded, lanes), f32),

time: 30.5 us -> 29.6 us (0.970)
  Pallas kernels: 29 us -> 28 us
    pallas_call x1, Pallas kernels: 29 us -> 28 us  [on_device(): pl.pallas_call(functools.partial(kernel, ny, nx), out_shape=jax.ShapeDtyp...]
where the time goes in v6:
time: 29.6 us; the launch traced here: 29.4 us
  Pallas kernels  28 us (95%)
  local copies, waits for them, and re-layouts  0.71 us (2%)
  between operations  0.66 us (2%)
    pallas_call x1, Pallas kernels, on_device(): pl.pallas_call(functools.partial(kernel, ny, nx), out_shape=jax.ShapeDtyp...  28 us
    unnamed x1, local copies, waits for them, and re-layouts  0.71 us

profile of v6, /device:TPU:0, one launch (start us, length us, event | category | flops | bytes accessed | tf_op | source)
XLA Modules:
  0.0 29.4 jit_solution(9262901851917289762)
XLA Ops:
  0.7 28.0 %shard_map.37 = f32[8,32,256]{2,1,0:T(8,128)S(1)} custom-call(f32[1]{0:T(128)S(6)} %copy.5.smooth_ref, f32[8,32,256]{2,1,0:T(8,128)} %vol_hbm.1, s32[2,4,32]{2,1,0:T(4,128)} %mask_hbm.1), custom_call_target="tpu_custom_call" | custom-call | tf_op jit(solution)/shard_map/pallas_call | solution.py:348
  28.7 0.7 %copy.6 = f32[8,32,256]{2,1,0:T(8,128)} copy(f32[8,32,256]{2,1,0:T(8,128)S(1)} %shard_map.37) | data formatting | bytes 524288
